TPU v7x, 32 devices: a whole 2x2x4 slice. The times are simulated.
32 devices in a mesh: row: 4 (over y, core), col: 8 (over z, x).
Axes of the slice: x: 2, y: 2, z: 4, core: 2. Of those that a mesh axis runs over, the one named last changes fastest.
Arguments:
- ancestor_inverse: float32 [12288, 12288], P('row', 'col')
- factor: bfloat16 [3, 12288, 512], P(None, ('row', 'col')), may hold values from -0.5 to 0.5
- coupling: float32 [3, 512, 512], replicated, may hold values from -0.25 to 0.25
- diagonal_inverse: float32 [3, 512, 512], replicated, may hold values from -6 to 6
- ancestors: int32 [3, 24], replicated, may hold values from -1 to 23, as said below
Outputs:
- block_columns: float32 [3, 12288, 512], P(None, ('row', 'col'))
- block_rows: float32 [3, 12288, 512], P(None, ('col', 'row'))
- node_blocks: float32 [3, 3, 512, 512], replicated
Inputs may be any that keep to these rules, and one draw needn't show every extreme that they name: `ancestors`: row k lists the ancestor block rows of supernode k, blocks of 512 rows: distinct indices in increasing order, then -1 in the slots left. Every block is listed by some supernode.
All inputs are finite; a program needn't handle non-finite values.
Results may differ from a plain program's by a relative error of at most 0.0003.
Values may be sent and summed in bfloat16 or wider, within the bound.
No kernel may reach another device: no remote copies, remote signals or barrier semaphores. Data moves between devices by JAX's collectives and lax.ppermute only.
A program may use at most 128 MiB of HBM per device.

v0:
```python
import jax
import jax.numpy as jnp
from jax import lax
from jax.sharding import PartitionSpec as P

highest = lax.Precision.HIGHEST


def broadcast(value, axis, source):
    kept = jnp.where(lax.axis_index(axis) == source, value, 0).astype(value.dtype)
    return lax.psum(kept, axis)


def matmul(left, right):
    return jnp.dot(left, right, precision=highest)


def left_dot(left, right):
    return lax.dot_general(left, right, (((0,), (0,)), ((), ())), precision=highest)


def pair_index(later, earlier):
    return later * (later - 1) // 2 + earlier


def local(ancestor_inverse, factor, coupling, diagonal_inverse, ancestors):
    col_count = lax.axis_size("col")
    row_index = lax.axis_index("row")
    col_index = lax.axis_index("col")
    nodes_total, piece_rows, sn_width = factor.shape
    rows_here, cols_here = ancestor_inverse.shape
    group_ratio = rows_here // cols_here
    first_row = (row_index * col_count + col_index) * piece_rows
    block_of_row = (first_row + jnp.arange(piece_rows, dtype=jnp.int32)) // sn_width
    source_row = col_index // group_ratio
    block_start = col_index % group_ratio * cols_here
    row_layout = []
    col_layout = []
    solved = {}
    for current in range(nodes_total):
        listed = jnp.any(ancestors[current][:, None] == block_of_row[None, :], axis=0)
        lower_part = jnp.where(listed[:, None], factor[current], jnp.zeros_like(factor[current]))
        lower_rows = lax.all_gather(lower_part, "col", axis=0, tiled=True)
        own_block = lax.dynamic_slice_in_dim(lower_rows, block_start, cols_here, 0)
        lower_cols = broadcast(own_block, "row", source_row).astype(jnp.float32)
        lower_here = lower_part.astype(jnp.float32)
        product_sum = lax.psum_scatter(
            matmul(ancestor_inverse, lower_cols), "col", scatter_dimension=0, tiled=True
        )
        for earlier in range(current):
            product_sum = product_sum + matmul(
                row_layout[earlier], coupling[pair_index(current, earlier)]
            )
        column = -product_sum
        stacked = jnp.concatenate(row_layout + [column], axis=1)
        summed = lax.psum(left_dot(lower_here, stacked), ("row", "col"))
        crosses = [
            summed[:, earlier * sn_width : (earlier + 1) * sn_width] for earlier in range(current)
        ]
        self_term = summed[:, current * sn_width : (current + 1) * sn_width]
        for earlier in range(current):
            block_value = -crosses[earlier].T
            for inner in range(current):
                block_value = block_value - matmul(
                    solved[earlier, inner], coupling[pair_index(current, inner)]
                )
            solved[earlier, current] = block_value
            solved[current, earlier] = block_value.T
        diag_value = diagonal_inverse[current] - self_term
        for earlier in range(current):
            diag_value = diag_value - left_dot(
                coupling[pair_index(current, earlier)], solved[earlier, current]
            )
        solved[current, current] = diag_value
        rows_float = lower_rows.astype(jnp.float32)
        mirror = lax.psum_scatter(
            left_dot(ancestor_inverse, rows_float), "row", scatter_dimension=0, tiled=True
        )
        for earlier in range(current):
            mirror = mirror + matmul(col_layout[earlier], coupling[pair_index(current, earlier)])
        col_layout.append(-mirror)
        row_layout.append(column)
    finished = jnp.stack(row_layout)
    mirrored_all = jnp.stack(col_layout)
    node_blocks = jnp.stack(
        [
            jnp.stack([solved[first_node, second_node] for second_node in range(nodes_total)])
            for first_node in range(nodes_total)
        ]
    )
    return (finished, mirrored_all, node_blocks)


def solution(mesh):
    placed = (P("row", "col"), P(None, ("row", "col"), None), P(), P(), P())
    return jax.shard_map(
        local,
        mesh=mesh,
        in_specs=placed,
        out_specs=(P(None, ("row", "col"), None), P(None, ("col", "row"), None), P()),
        check_vma=False,
    )
```

profile of v0, /device:TPU:0, one launch (start us, length us, event | category | flops | bytes accessed | tf_op | source)
XLA Modules:
  0.0 1007.5 jit_solution(5974017174490358877)
XLA Ops:
  7.2 0.8 slice_bitcast_fusion.2
  8.1 2.5 bitcast_select_fusion.1
  10.7 0.7 all-gather.4.cloned.1.call-update
  11.5 0.7 all-gather.6.cloned.1.call-update
  12.2 61.3 %all-gather.8.cloned.1.call-done = bf16[3072,512]{1,0:T(8,128)(2,1)} async-done(((bf16[384,512]{1,0:T(8,128)(2,1)}), bf16[3072,512]{1,0:T(8,128)(2,1)}) %all-gather.8.cloned.1.call-update) | async-done | bytes 3145744 | tf_op jit(solution)/shard_map/all_gather | solution.py:43
  73.6 2.8 dynamic-slice_select_fusion
  76.4 58.1 %all-gather.4.cloned.1.call-done = bf16[3072,512]{1,0:T(8,128)(2,1)} async-done(((bf16[384,512]{1,0:T(8,128)(2,1)}), bf16[3072,512]{1,0:T(8,128)(2,1)}) %all-gather.4.cloned.1.call-update) | async-done | bytes 3145744 | tf_op jit(solution)/shard_map/all_gather | solution.py:43
  134.5 2.8 dynamic-slice_select_fusion.2
  137.3 58.1 %all-gather.6.cloned.1.call-done = bf16[3072,512]{1,0:T(8,128)(2,1)} async-done(((bf16[384,512]{1,0:T(8,128)(2,1)}), bf16[3072,512]{1,0:T(8,128)(2,1)}) %all-gather.6.cloned.1.call-update) | async-done | bytes 3145744 | tf_op jit(solution)/shard_map/all_gather | solution.py:43
  195.4 2.8 dynamic-slice_select_fusion.1
  198.3 92.8 %all-reduce.7.cloned.1.call-done = (bf16[1536,512]{1,0:T(8,128)(2,1)}, bf16[1536,512]{1,0:T(8,128)(2,1)}, bf16[1536,512]{1,0:T(8,128)(2,1)}) async-done(((bf16[1536,512]{1,0:T(8,128)(2,1)}, bf16[1536,512]{1,0:T(8,128)(2,1)}, bf16[1536,512]{1,0:T(8,128)(2,1)}), (bf16[1536,512]{1,0:T(8,128)(2,1)}, bf16[1536,512]{1,0:T(8,128)(2,1)}, bf16[1536,512]{1,0:T(8,128)(2,1)})) %all-reduce.7.cloned.1.call-update) | async-done | bytes 4718608 | tf_op jit(solution)/shard_map/psum | solution.py:11
  291.1 22.4 %convolution_bitcast_fusion.2 = f32[3072,512]{0,1:T(8,128)} fusion(bf16[1536,512]{1,0:T(8,128)(2,1)} %get-tuple-element.16, f32[3072,1536]{1,0:T(8,128)} %param.5), kind=kOutput, calls=%fused_computation.3 | convolution fusion | flops 28991029248 | bytes 26738688 | tf_op jit(solution)/shard_map/dot_general | solution.py:15
  313.5 1.3 copy-done.30
  314.9 21.8 %convolution_bitcast_fusion.1 = f32[3072,512]{0,1:T(8,128)} fusion(bf16[1536,512]{1,0:T(8,128)(2,1)S(1)} %copy-done.30, f32[3072,1536]{1,0:T(8,128)} %param.5), kind=kOutput, calls=%fused_computation.2 | convolution fusion | flops 28991029248 | bytes 26738688 | tf_op jit(solution)/shard_map/dot_general | solution.py:15
  336.7 0.5 reduce-scatter.11.cloned.1.call-start
  337.2 0.9 copy-done.29
  338.1 21.8 %convolution_bitcast_fusion = f32[3072,512]{0,1:T(8,128)} fusion(bf16[1536,512]{1,0:T(8,128)(2,1)S(1)} %copy-done.29, f32[3072,1536]{1,0:T(8,128)} %param.5), kind=kOutput, calls=%fused_computation.1 | convolution fusion | flops 28991029248 | bytes 26738688 | tf_op jit(solution)/shard_map/dot_general | solution.py:15
  360.0 1.9 copy-done.28
  361.8 19.7 %convolution_bitcast_fusion.3 = f32[1536,512]{0,1:T(8,128)} fusion(bf16[3072,512]{1,0:T(8,128)(2,1)S(1)} %copy-done.28, f32[3072,1536]{1,0:T(8,128)} %param.5), kind=kOutput, calls=%fused_computation.4 | convolution fusion | flops 28991029248 | bytes 25165824 | tf_op jit(solution)/shard_map/dot_general | solution.py:19
  381.8 1.7 copy-done.27
  383.5 19.9 %convolution_bitcast_fusion.5 = f32[1536,512]{0,1:T(8,128)} fusion(bf16[3072,512]{1,0:T(8,128)(2,1)S(1)} %copy-done.27, f32[3072,1536]{1,0:T(8,128)} %param.5), kind=kOutput, calls=%fused_computation.6 | convolution fusion | flops 28991029248 | bytes 25165824 | tf_op jit(solution)/shard_map/dot_general | solution.py:19
  403.5 1.8 copy-done.26
  405.3 19.7 %convolution_bitcast_fusion.4 = f32[1536,512]{0,1:T(8,128)} fusion(bf16[3072,512]{1,0:T(8,128)(2,1)S(1)} %copy-done.26, f32[3072,1536]{1,0:T(8,128)} %param.5), kind=kOutput, calls=%fused_computation.5 | convolution fusion | flops 28991029248 | bytes 25165824 | tf_op jit(solution)/shard_map/dot_general | solution.py:19
  425.3 6.5 reduce-scatter.7.cloned.1.call-done
  431.8 2.4 fusion.73
  434.2 3.3 fusion.64
  437.5 115.1 %reduce-scatter.9.cloned.1.call-done = f32[384,512]{0,1:T(8,128)} async-done(((f32[3072,512]{0,1:T(8,128)}), f32[384,512]{0,1:T(8,128)}) %reduce-scatter.9.cloned.1.call-update) | async-done | bytes 786448 | tf_op jit(solution)/shard_map/reduce_scatter | solution.py:47
  552.6 3.4 fusion.14
  555.9 0.9 copy-done.3
  556.9 3.1 fusion.6
  560.0 114.0 %reduce-scatter.11.cloned.1.call-done = f32[384,512]{0,1:T(8,128)} async-done(((f32[3072,512]{0,1:T(8,128)}), f32[384,512]{0,1:T(8,128)}) %reduce-scatter.11.cloned.1.call-update) | async-done | bytes 786448 | tf_op jit(solution)/shard_map/reduce_scatter | solution.py:47
  674.0 3.3 convolution_add_fusion.4
  677.4 1.9 fusion.15
  679.3 0.9 copy-done.12
  680.2 4.5 fusion
  684.7 2.3 slice.74
  687.0 2.9 copy.65
  690.0 23.6 %reduce-scatter.17.cloned.1.call-done = f32[384,512]{0,1:T(8,128)} async-done(((f32[1536,512]{0,1:T(8,128)}), f32[384,512]{0,1:T(8,128)}) %reduce-scatter.17.cloned.1.call-update) | async-done | bytes 786448 | tf_op jit(solution)/shard_map/reduce_scatter | solution.py:76
  713.6 40.3 %reduce-scatter.13.cloned.1.call-done = f32[384,512]{0,1:T(8,128)} async-done(((f32[1536,512]{0,1:T(8,128)}), f32[384,512]{0,1:T(8,128)}) %reduce-scatter.13.cloned.1.call-update) | async-done | bytes 786448 | tf_op jit(solution)/shard_map/reduce_scatter | solution.py:76
  753.9 4.1 convolution_add_fusion.1
  758.0 36.0 %reduce-scatter.15.cloned.1.call-done = f32[384,512]{0,1:T(8,128)} async-done(((f32[1536,512]{0,1:T(8,128)}), f32[384,512]{0,1:T(8,128)}) %reduce-scatter.15.cloned.1.call-update) | async-done | bytes 786448 | tf_op jit(solution)/shard_map/reduce_scatter | solution.py:76
  794.0 3.4 fusion.16
  797.4 1.9 fusion.18
  799.4 1.6 pad_maximum_fusion.2
  800.9 3.0 copy.51
  804.0 3.2 pad_maximum_fusion.1
  807.1 3.2 copy.50
  810.3 146.5 %all-reduce.5.cloned.1.call-done = (f32[512,1536]{1,0:T(8,128)}, f32[512,512]{1,0:T(8,128)}, f32[512,1024]{0,1:T(8,128)}) async-done(((f32[512,1536]{1,0:T(8,128)}, f32[512,512]{1,0:T(8,128)}, f32[512,1024]{0,1:T(8,128)}), (f32[512,1536]{1,0:T(8,128)}, f32[512,512]{1,0:T(8,128)}, f32[512,1024]{0,1:T(8,128)})) %all-reduce.5.cloned.1.call-update) | async-done | bytes 6291472 | tf_op jit(solution)/shard_map/psum | solution.py:56
  956.9 3.6 fusion.34
  960.5 3.2 bitcast_subtract_fusion.7
  963.7 1.9 fusion.32
  965.6 1.9 fusion.27
  967.5 2.0 fusion.13
  969.5 1.0 copy-done.8
  970.5 1.9 fusion.25
  972.4 3.3 fusion.12
  975.7 2.3 fusion.20
  978.0 2.3 fusion.70
  980.3 2.5 copy.39
  982.9 5.3 fusion.11
  988.2 2.0 maximum_bitcast_fusion.1
  990.1 2.4 copy.49
  992.6 2.3 maximum_bitcast_fusion.2
  995.6 5.1 pad_maximum_fusion
  (77 shorter events, 1.9 us)
Async XLA Ops:
  7.2 66.4 %all-gather.8.cloned.1.call-start = ((), (), s32[]{:S(2)}) async-start(), calls=%async_computation.10 | async-start | bytes 3538944 | tf_op jit(solution)/shard_map/all_gather | solution.py:43
  10.7 123.8 %all-gather.4.cloned.1.call-start = ((), (), s32[]{:S(2)}) async-start(), calls=%async_computation.6 | async-start | bytes 3538944 | tf_op jit(solution)/shard_map/all_gather | solution.py:43
  11.4 183.9 %all-gather.6.cloned.1.call-start = ((), (), s32[]{:S(2)}) async-start(), calls=%async_computation.8 | async-start | bytes 3538944 | tf_op jit(solution)/shard_map/all_gather | solution.py:43
  12.2 278.9 %all-reduce.7.cloned.1.call-start = ((), (), s32[]{:S(2)}) async-start(), calls=%async_computation.16 | async-start | bytes 9437184 | tf_op jit(solution)/shard_map/psum | solution.py:11
  198.2 233.6 %reduce-scatter.7.cloned.1.call-start = ((), (), s32[]{:S(2)}) async-start(), calls=%async_computation.7 | async-start | bytes 7077888 | tf_op jit(solution)/shard_map/reduce_scatter | solution.py:47
  313.5 1.4 copy-start.30
  313.5 239.1 %reduce-scatter.9.cloned.1.call-start = ((), (), s32[]{:S(2)}) async-start(), calls=%async_computation.9 | async-start | bytes 7077888 | tf_op jit(solution)/shard_map/reduce_scatter | solution.py:47
  336.7 1.4 copy-start.29
  336.7 337.3 %reduce-scatter.11.cloned.1.call-start = ((), (), s32[]{:S(2)}) async-start(), calls=%async_computation.11 | async-start | bytes 7077888 | tf_op jit(solution)/shard_map/reduce_scatter | solution.py:47
  359.9 1.9 copy-start.28
  359.9 353.6 %reduce-scatter.17.cloned.1.call-start = ((), (), s32[]{:S(2)}) async-start(), calls=%async_computation.14 | async-start | bytes 3932160 | tf_op jit(solution)/shard_map/reduce_scatter | solution.py:76
  381.6 2.0 copy-start.27
  381.6 372.2 %reduce-scatter.13.cloned.1.call-start = ((), (), s32[]{:S(2)}) async-start(), calls=%async_computation.12 | async-start | bytes 3932160 | tf_op jit(solution)/shard_map/reduce_scatter | solution.py:76
  403.4 1.9 copy-start.26
  403.5 390.5 %reduce-scatter.15.cloned.1.call-start = ((), (), s32[]{:S(2)}) async-start(), calls=%async_computation.13 | async-start | bytes 3932160 | tf_op jit(solution)/shard_map/reduce_scatter | solution.py:76
  425.0 9.2 copy-start.23
  425.0 127.6 %copy-start = (f32[3,512,512]{2,1,0:T(8,128)S(1)}, f32[3,512,512]{2,1,0:T(8,128)}, u32[]{:S(2)}) copy-start(f32[3,512,512]{2,1,0:T(8,128)} %param.7) | copy-start | bytes 9437188
  425.0 531.9 %all-reduce.5.cloned.1.call-start = ((), (), s32[]{:S(2)}) async-start(), calls=%async_computation.15 | async-start | bytes 12582912 | tf_op jit(solution)/shard_map/psum | solution.py:56
  437.5 119.4 %copy-start.24 = (bf16[384,512]{1,0:T(8,128)(2,1)S(1)}, bf16[384,512]{1,0:T(8,128)(2,1)}, u32[]{:S(2)}) copy-start(bf16[384,512]{1,0:T(8,128)(2,1)} %get-tuple-element.22) | copy-start | bytes 1179652
  552.6 4.3 copy-start.13
  555.9 0.9 copy-start.3
  560.0 120.2 %copy-start.16 = (bf16[384,512]{1,0:T(8,128)(2,1)S(1)}, bf16[384,512]{1,0:T(8,128)(2,1)}, u32[]{:S(2)}) copy-start(bf16[384,512]{1,0:T(8,128)(2,1)} %get-tuple-element.24) | copy-start | bytes 1179652
  674.0 3.4 copy-start.4
  674.0 6.2 copy-start.14
  679.2 0.9 copy-start.12
  794.0 3.4 copy-start.25
  794.0 5.3 copy-start.15
  956.9 3.6 copy-start.10
  956.9 3.6 copy-start.11
  963.7 3.8 copy-start.1
  963.7 3.8 copy-start.17
  963.7 3.8 copy-start.18
  965.6 12.4 %copy-start.5 = (f32[512,512]{0,1:T(8,128)}, f32[512,512]{0,1:T(8,128)S(1)}, u32[]{:S(2)}) copy-start(f32[512,512]{0,1:T(8,128)S(1)} %fusion.32) | copy-start | bytes 3145732
  967.5 4.9 copy-start.7
  969.5 1.0 copy-start.8
  972.4 5.6 copy-start.6
  982.9 5.3 copy-start.9
  982.9 5.3 copy-start.21
  982.9 5.3 copy-start.22
  992.5 2.4 copy-start.2
  992.5 2.5 copy-start.19
  992.5 2.8 copy-start.20
Sparse Core Ops, SparseCore 0:
  10.8 62.7 all-gather.7
  75.7 58.6 all-gather.3
  136.7 58.6 all-gather.5
  198.3 92.7 all-reduce.6
  313.6 118.1 reduce-scatter.6
  435.2 117.2 reduce-scatter.8
  556.7 117.2 reduce-scatter.10
  676.5 36.9 reduce-scatter.16
  716.1 37.7 reduce-scatter.12
  756.2 37.7 reduce-scatter.14
  800.5 156.3 all-reduce.4
where the time goes:
time: 1020 us; the launch traced here: 1010 us
  waiting for transfers between devices  754 us (74%)
  matrix products  177 us (17%)
  other arithmetic  32.6 us (3%)
  local copies, waits for them, and re-layouts  28.1 us (3%)
  between operations  14.5 us (1%)
    reduce_scatter x3, waiting for transfers between devices, local(): lax.psum_scatter(matmul(ancestor_inverse, lower_cols), 'col', scatter_dim...  236 us
    all_gather x3, waiting for transfers between devices, local(): lower_rows = lax.all_gather(lower_part, 'col', axis=0, tiled=True)  177 us
    psum x1, waiting for transfers between devices, local(): summed = lax.psum(left_dot(lower_here, stacked), ('row', 'col'))  147 us
    reduce_scatter x3, waiting for transfers between devices, local(): lax.psum_scatter(left_dot(ancestor_inverse, rows_float), 'row', scatter_d...  99.9 us
    dot_general x14, matrix products, matmul(): return jnp.dot(left, right, precision=highest)  96.3 us
    psum x1, waiting for transfers between devices, broadcast(): return lax.psum(kept, axis)  92.8 us
    dot_general x9, matrix products, left_dot(): lax.dot_general(left, right, (((0,), (0,)), ((), ())), precision=highest)  80.7 us
  transfers between devices with their start and end apart: 11, of which 11 were waited for; matrix products, arithmetic and copies ran while one was open for 15% of the time, Pallas kernels for 0%

commit v1 on v0

--- a/solution.py
+++ b/solution.py
@@ -6,9 +6,15 @@
 highest = lax.Precision.HIGHEST
 
 
+def gather_and_add(x, axis):
+    parts = lax.all_gather(x, axis, axis=0, tiled=False)
+    acc = parts.sum(axis=0)
+    return acc
+
+
 def broadcast(value, axis, source):
     kept = jnp.where(lax.axis_index(axis) == source, value, 0).astype(value.dtype)
-    return lax.psum(kept, axis)
+    return gather_and_add(kept, axis)
 
 
 def matmul(left, right):

time: 1020 us -> 1040 us (1.020)
  waiting for transfers between devices: 754 us -> 771 us
  other arithmetic: 32.6 us -> 47.2 us
    psum x1 -> x0, waiting for transfers between devices: 92.8 us -> none  [broadcast(): return lax.psum(kept, axis)]
    all_gather x0 -> x3, waiting for transfers between devices: none -> 86.7 us  [gather_and_add(): parts = lax.all_gather(x, axis, axis=0, tiled=False)]
    reduce_scatter x3, waiting for transfers between devices: 236 us -> 259 us  [local(): lax.psum_scatter(matmul(ancestor_inverse, lower_cols), 'col', scatter_dim...]
    reduce_sum x0 -> x3, other arithmetic: none -> 14.5 us  [gather_and_add(): acc = parts.sum(axis=0)]
  transfers between devices with their start and end apart: 11 -> 13, of which waited for: 11 -> 13; matrix products, arithmetic and copies ran while one was open for 15% -> 19% of each run, Pallas kernels for 0% -> 0%
where the time goes in v1:
time: 1040 us
  waiting for transfers between devices  771 us (74%)
  matrix products  177 us (17%)
  other arithmetic  47.2 us (5%)
  local copies, waits for them, and re-layouts  25.3 us (2%)
  between operations  14.7 us (1%)
    reduce_scatter x3, waiting for transfers between devices, local(): lax.psum_scatter(matmul(ancestor_inverse, lower_cols), 'col', scatter_dim...  259 us
    all_gather x3, waiting for transfers between devices, local(): lower_rows = lax.all_gather(lower_part, 'col', axis=0, tiled=True)  177 us
    psum x1, waiting for transfers between devices, local(): summed = lax.psum(left_dot(lower_here, stacked), ('row', 'col'))  146 us
    reduce_scatter x3, waiting for transfers between devices, local(): lax.psum_scatter(left_dot(ancestor_inverse, rows_float), 'row', scatter_d...  100 us
    dot_general x14, matrix products, matmul(): return jnp.dot(left, right, precision=highest)  95.9 us
    all_gather x3, waiting for transfers between devices, gather_and_add(): parts = lax.all_gather(x, axis, axis=0, tiled=False)  86.7 us
    dot_general x9, matrix products, left_dot(): lax.dot_general(left, right, (((0,), (0,)), ((), ())), precision=highest)  80.9 us
  transfers between devices with their start and end apart: 13, of which 13 were waited for; matrix products, arithmetic and copies ran while one was open for 19% of the time, Pallas kernels for 0%

profile of v1, /device:TPU:0, one launch (start us, length us, event | category | flops | bytes accessed | tf_op | source)
XLA Modules:
  0.0 1036.9 jit_solution(1162040543523967988)
XLA Ops:
  7.2 0.8 slice_bitcast_fusion.2
  8.1 2.5 bitcast_select_fusion.1
  12.2 61.3 %all-gather.10.cloned.1.call-done = bf16[3072,512]{1,0:T(8,128)(2,1)} async-done(((bf16[384,512]{1,0:T(8,128)(2,1)}), bf16[3072,512]{1,0:T(8,128)(2,1)}) %all-gather.10.cloned.1.call-update) | async-done | bytes 3145744 | tf_op jit(solution)/shard_map/all_gather | solution.py:49
  73.5 2.8 dynamic-slice_select_fusion.2
  76.4 58.0 %all-gather.12.cloned.1.call-done = bf16[3072,512]{1,0:T(8,128)(2,1)} async-done(((bf16[384,512]{1,0:T(8,128)(2,1)}), bf16[3072,512]{1,0:T(8,128)(2,1)}) %all-gather.12.cloned.1.call-update) | async-done | bytes 3145744 | tf_op jit(solution)/shard_map/all_gather | solution.py:49
  134.4 2.8 dynamic-slice_select_fusion.1
  137.3 58.0 %all-gather.14.cloned.1.call-done = bf16[3072,512]{1,0:T(8,128)(2,1)} async-done(((bf16[384,512]{1,0:T(8,128)(2,1)}), bf16[3072,512]{1,0:T(8,128)(2,1)}) %all-gather.14.cloned.1.call-update) | async-done | bytes 3145744 | tf_op jit(solution)/shard_map/all_gather | solution.py:49
  195.3 2.8 dynamic-slice_select_fusion
  198.2 44.2 %all-gather.16.cloned.1.call-done = bf16[6144,512]{1,0:T(8,128)(2,1)} async-done(((bf16[1536,512]{1,0:T(8,128)(2,1)}), bf16[6144,512]{1,0:T(8,128)(2,1)}) %all-gather.16.cloned.1.call-update) | async-done | bytes 6291472 | tf_op jit(solution)/shard_map/all_gather | solution.py:10
  242.4 4.8 reduce_sum.36
  247.2 21.9 %convolution_bitcast_fusion.2 = f32[3072,512]{0,1:T(8,128)} fusion(bf16[1536,512]{1,0:T(8,128)(2,1)S(1)} %reduce_sum.36, f32[3072,1536]{1,0:T(8,128)} %param.5), kind=kOutput, calls=%fused_computation.3 | convolution fusion | flops 28991029248 | bytes 26738688 | tf_op jit(solution)/shard_map/dot_general | solution.py:21
  269.7 21.1 %all-gather.18.cloned.1.call-done = bf16[6144,512]{1,0:T(8,128)(2,1)} async-done(((bf16[1536,512]{1,0:T(8,128)(2,1)}), bf16[6144,512]{1,0:T(8,128)(2,1)}) %all-gather.18.cloned.1.call-update) | async-done | bytes 6291472 | tf_op jit(solution)/shard_map/all_gather | solution.py:10
  290.8 4.8 reduce_sum.37
  295.6 21.9 %convolution_bitcast_fusion.1 = f32[3072,512]{0,1:T(8,128)} fusion(bf16[1536,512]{1,0:T(8,128)(2,1)S(1)} %reduce_sum.37, f32[3072,1536]{1,0:T(8,128)} %param.5), kind=kOutput, calls=%fused_computation.2 | convolution fusion | flops 28991029248 | bytes 26738688 | tf_op jit(solution)/shard_map/dot_general | solution.py:21
  317.7 21.4 %all-gather.20.cloned.1.call-done = bf16[6144,512]{1,0:T(8,128)(2,1)} async-done(((bf16[1536,512]{1,0:T(8,128)(2,1)}), bf16[6144,512]{1,0:T(8,128)(2,1)}) %all-gather.20.cloned.1.call-update) | async-done | bytes 6291472 | tf_op jit(solution)/shard_map/all_gather | solution.py:10
  339.1 4.8 reduce_sum.38
  344.0 21.8 %convolution_bitcast_fusion = f32[3072,512]{0,1:T(8,128)} fusion(bf16[1536,512]{1,0:T(8,128)(2,1)S(1)} %reduce_sum.38, f32[3072,1536]{1,0:T(8,128)} %param.5), kind=kOutput, calls=%fused_computation.1 | convolution fusion | flops 28991029248 | bytes 26738688 | tf_op jit(solution)/shard_map/dot_general | solution.py:21
  366.0 1.7 copy-done.28
  367.7 19.7 %convolution_bitcast_fusion.3 = f32[1536,512]{0,1:T(8,128)} fusion(bf16[3072,512]{1,0:T(8,128)(2,1)S(1)} %copy-done.28, f32[3072,1536]{1,0:T(8,128)} %param.5), kind=kOutput, calls=%fused_computation.4 | convolution fusion | flops 28991029248 | bytes 25165824 | tf_op jit(solution)/shard_map/dot_general | solution.py:25
  387.5 1.8 copy-done.27
  389.4 19.7 %convolution_bitcast_fusion.5 = f32[1536,512]{0,1:T(8,128)} fusion(bf16[3072,512]{1,0:T(8,128)(2,1)S(1)} %copy-done.27, f32[3072,1536]{1,0:T(8,128)} %param.5), kind=kOutput, calls=%fused_computation.6 | convolution fusion | flops 28991029248 | bytes 25165824 | tf_op jit(solution)/shard_map/dot_general | solution.py:25
  409.6 1.5 copy-done.26
  411.0 19.9 %convolution_bitcast_fusion.4 = f32[1536,512]{0,1:T(8,128)} fusion(bf16[3072,512]{1,0:T(8,128)(2,1)S(1)} %copy-done.26, f32[3072,1536]{1,0:T(8,128)} %param.5), kind=kOutput, calls=%fused_computation.5 | convolution fusion | flops 28991029248 | bytes 25165824 | tf_op jit(solution)/shard_map/dot_general | solution.py:25
  431.1 29.7 %reduce-scatter.7.cloned.1.call-done = f32[384,512]{0,1:T(8,128)} async-done(((f32[3072,512]{0,1:T(8,128)}), f32[384,512]{0,1:T(8,128)}) %reduce-scatter.7.cloned.1.call-update) | async-done | bytes 786448 | tf_op jit(solution)/shard_map/reduce_scatter | solution.py:53
  460.8 2.4 fusion.73
  463.2 3.2 fusion.64
  466.4 115.2 %reduce-scatter.9.cloned.1.call-done = f32[384,512]{0,1:T(8,128)} async-done(((f32[3072,512]{0,1:T(8,128)}), f32[384,512]{0,1:T(8,128)}) %reduce-scatter.9.cloned.1.call-update) | async-done | bytes 786448 | tf_op jit(solution)/shard_map/reduce_scatter | solution.py:53
  581.6 3.4 fusion.14
  585.0 0.9 copy-done.3
  585.9 3.1 fusion.6
  589.0 114.1 %reduce-scatter.11.cloned.1.call-done = f32[384,512]{0,1:T(8,128)} async-done(((f32[3072,512]{0,1:T(8,128)}), f32[384,512]{0,1:T(8,128)}) %reduce-scatter.11.cloned.1.call-update) | async-done | bytes 786448 | tf_op jit(solution)/shard_map/reduce_scatter | solution.py:53
  703.1 3.3 convolution_add_fusion.4
  706.5 1.9 fusion.15
  708.4 0.9 copy-done.12
  709.2 4.5 fusion
  713.8 2.3 slice.74
  716.1 2.7 copy.65
  718.8 23.7 %reduce-scatter.17.cloned.1.call-done = f32[384,512]{0,1:T(8,128)} async-done(((f32[1536,512]{0,1:T(8,128)}), f32[384,512]{0,1:T(8,128)}) %reduce-scatter.17.cloned.1.call-update) | async-done | bytes 786448 | tf_op jit(solution)/shard_map/reduce_scatter | solution.py:82
  742.5 40.3 %reduce-scatter.13.cloned.1.call-done = f32[384,512]{0,1:T(8,128)} async-done(((f32[1536,512]{0,1:T(8,128)}), f32[384,512]{0,1:T(8,128)}) %reduce-scatter.13.cloned.1.call-update) | async-done | bytes 786448 | tf_op jit(solution)/shard_map/reduce_scatter | solution.py:82
  782.8 4.1 convolution_add_fusion.1
  786.9 36.0 %reduce-scatter.15.cloned.1.call-done = f32[384,512]{0,1:T(8,128)} async-done(((f32[1536,512]{0,1:T(8,128)}), f32[384,512]{0,1:T(8,128)}) %reduce-scatter.15.cloned.1.call-update) | async-done | bytes 786448 | tf_op jit(solution)/shard_map/reduce_scatter | solution.py:82
  823.0 3.4 fusion.16
  826.4 1.9 fusion.18
  828.3 1.6 pad_maximum_fusion.2
  829.9 3.0 copy.51
  833.0 3.2 pad_maximum_fusion.1
  836.1 3.2 copy.50
  839.4 146.4 %all-reduce.3.cloned.1.call-done = (f32[512,1536]{1,0:T(8,128)}, f32[512,512]{1,0:T(8,128)}, f32[512,1024]{0,1:T(8,128)}) async-done(((f32[512,1536]{1,0:T(8,128)}, f32[512,512]{1,0:T(8,128)}, f32[512,1024]{0,1:T(8,128)}), (f32[512,1536]{1,0:T(8,128)}, f32[512,512]{1,0:T(8,128)}, f32[512,1024]{0,1:T(8,128)})) %all-reduce.3.cloned.1.call-update) | async-done | bytes 6291472 | tf_op jit(solution)/shard_map/psum | solution.py:62
  985.8 3.6 fusion.34
  989.4 3.2 bitcast_subtract_fusion.7
  992.6 1.9 fusion.32
  994.5 1.9 fusion.27
  996.5 2.0 fusion.13
  998.4 1.1 copy-done.8
  999.5 1.9 fusion.25
  1001.4 3.3 fusion.12
  1004.7 2.4 fusion.20
  1007.1 2.4 fusion.70
  1009.5 2.6 copy.39
  1012.0 5.3 fusion.11
  1017.4 2.0 maximum_bitcast_fusion.1
  1019.4 2.4 copy.49
  1021.8 2.3 maximum_bitcast_fusion.2
  1024.9 5.1 pad_maximum_fusion
  (82 shorter events, 4.4 us)
Async XLA Ops:
  7.2 66.4 %all-gather.10.cloned.1.call-start = ((), (), s32[]{:S(2)}) async-start(), calls=%async_computation.6 | async-start | bytes 3538944 | tf_op jit(solution)/shard_map/all_gather | solution.py:49
  10.7 123.8 %all-gather.12.cloned.1.call-start = ((), (), s32[]{:S(2)}) async-start(), calls=%async_computation.8 | async-start | bytes 3538944 | tf_op jit(solution)/shard_map/all_gather | solution.py:49
  11.4 183.9 %all-gather.14.cloned.1.call-start = ((), (), s32[]{:S(2)}) async-start(), calls=%async_computation.10 | async-start | bytes 3538944 | tf_op jit(solution)/shard_map/all_gather | solution.py:49
  12.1 230.2 %all-gather.16.cloned.1.call-start = ((), (), s32[]{:S(2)}) async-start(), calls=%async_computation.15 | async-start | bytes 7864320 | tf_op jit(solution)/shard_map/all_gather | solution.py:10
  76.4 214.4 %all-gather.18.cloned.1.call-start = ((), (), s32[]{:S(2)}) async-start(), calls=%async_computation.16 | async-start | bytes 7864320 | tf_op jit(solution)/shard_map/all_gather | solution.py:10
  137.3 201.9 %all-gather.20.cloned.1.call-start = ((), (), s32[]{:S(2)}) async-start(), calls=%async_computation.17 | async-start | bytes 7864320 | tf_op jit(solution)/shard_map/all_gather | solution.py:10
  198.2 262.6 %reduce-scatter.7.cloned.1.call-start = ((), (), s32[]{:S(2)}) async-start(), calls=%async_computation.7 | async-start | bytes 7077888 | tf_op jit(solution)/shard_map/reduce_scatter | solution.py:53
  269.1 312.5 %reduce-scatter.9.cloned.1.call-start = ((), (), s32[]{:S(2)}) async-start(), calls=%async_computation.9 | async-start | bytes 7077888 | tf_op jit(solution)/shard_map/reduce_scatter | solution.py:53
  317.5 385.6 %reduce-scatter.11.cloned.1.call-start = ((), (), s32[]{:S(2)}) async-start(), calls=%async_computation.11 | async-start | bytes 7077888 | tf_op jit(solution)/shard_map/reduce_scatter | solution.py:53
  365.7 1.9 copy-start.28
  365.8 376.7 %reduce-scatter.17.cloned.1.call-start = ((), (), s32[]{:S(2)}) async-start(), calls=%async_computation.14 | async-start | bytes 3932160 | tf_op jit(solution)/shard_map/reduce_scatter | solution.py:82
  387.4 1.9 copy-start.27
  387.5 395.4 %reduce-scatter.13.cloned.1.call-start = ((), (), s32[]{:S(2)}) async-start(), calls=%async_computation.12 | async-start | bytes 3932160 | tf_op jit(solution)/shard_map/reduce_scatter | solution.py:82
  409.1 1.9 copy-start.26
  409.1 413.9 %reduce-scatter.15.cloned.1.call-start = ((), (), s32[]{:S(2)}) async-start(), calls=%async_computation.13 | async-start | bytes 3932160 | tf_op jit(solution)/shard_map/reduce_scatter | solution.py:82
  431.0 32.2 %copy-start.23 = (bf16[384,512]{1,0:T(8,128)(2,1)S(1)}, bf16[384,512]{1,0:T(8,128)(2,1)}, u32[]{:S(2)}) copy-start(bf16[384,512]{1,0:T(8,128)(2,1)} %get-tuple-element.20) | copy-start | bytes 1179652
  431.0 150.7 %copy-start = (f32[3,512,512]{2,1,0:T(8,128)S(1)}, f32[3,512,512]{2,1,0:T(8,128)}, u32[]{:S(2)}) copy-start(f32[3,512,512]{2,1,0:T(8,128)} %param.7) | copy-start | bytes 9437188
  431.0 554.8 %all-reduce.3.cloned.1.call-start = ((), (), s32[]{:S(2)}) async-start(), calls=%async_computation.18 | async-start | bytes 12582912 | tf_op jit(solution)/shard_map/psum | solution.py:62
  466.4 119.5 %copy-start.24 = (bf16[384,512]{1,0:T(8,128)(2,1)S(1)}, bf16[384,512]{1,0:T(8,128)(2,1)}, u32[]{:S(2)}) copy-start(bf16[384,512]{1,0:T(8,128)(2,1)} %get-tuple-element.19) | copy-start | bytes 1179652
  581.6 4.2 copy-start.13
  585.0 0.9 copy-start.3
  589.0 120.2 %copy-start.16 = (bf16[384,512]{1,0:T(8,128)(2,1)S(1)}, bf16[384,512]{1,0:T(8,128)(2,1)}, u32[]{:S(2)}) copy-start(bf16[384,512]{1,0:T(8,128)(2,1)} %get-tuple-element.21) | copy-start | bytes 1179652
  703.1 3.4 copy-start.4
  703.1 6.1 copy-start.14
  708.4 0.9 copy-start.12
  823.0 3.4 copy-start.25
  823.0 5.3 copy-start.15
  985.8 3.6 copy-start.10
  985.8 3.6 copy-start.11
  992.6 3.8 copy-start.1
  992.6 3.8 copy-start.17
  992.6 3.8 copy-start.18
  994.5 12.6 %copy-start.5 = (f32[512,512]{0,1:T(8,128)}, f32[512,512]{0,1:T(8,128)S(1)}, u32[]{:S(2)}) copy-start(f32[512,512]{0,1:T(8,128)S(1)} %fusion.32) | copy-start | bytes 3145732
  996.4 5.0 copy-start.7
  998.4 1.1 copy-start.8
  1001.4 5.7 copy-start.6
  1012.0 5.3 copy-start.9
  1012.0 5.3 copy-start.21
  1012.0 5.3 copy-start.22
  1021.7 2.4 copy-start.2
  1021.8 2.5 copy-start.19
  1021.8 2.8 copy-start.20
Sparse Core Ops, SparseCore 0:
  10.8 62.7 all-gather.9
  75.7 58.6 all-gather.11
  136.6 58.6 all-gather.13
  197.3 45.0 all-gather.15
  244.4 46.3 all-gather.17
  292.8 46.3 all-gather.19
  342.7 117.9 reduce-scatter.6
  464.3 117.2 reduce-scatter.8
  585.8 117.2 reduce-scatter.10
  705.5 36.9 reduce-scatter.16
  745.1 37.7 reduce-scatter.12
  785.2 37.7 reduce-scatter.14
  829.5 156.2 all-reduce.2
